TPU v7x, 32 devices: a whole 2x2x4 slice. The times are simulated.
32 devices in a mesh: row: 4 (over z), col: 8 (over y, x, core).
Axes of the slice: x: 2, y: 2, z: 4, core: 2. Of those that a mesh axis runs over, the one named last changes fastest.
Arguments:
- customer_inputs: bfloat16 [32768, 1024], P(('row', 'col')), may hold values from -6 to 6
- candidate_inputs: bfloat16 [32768, 1024], P(('row', 'col')), may hold values from -6 to 6
- affinity_sharpness: bfloat16 [32768], P(('row', 'col')), may hold values from 4 to 40
- correct_candidate_index: int32 [32768], P(('row', 'col')), may hold values from 0 to 4095
- customer_initial_weights: bfloat16 [1024, 512], replicated, may hold values from -0.1875 to 0.1875
- customer_final_weights: bfloat16 [512, 256], replicated, may hold values from -0.25 to 0.25
- candidate_initial_weights: bfloat16 [1024, 512], replicated, may hold values from -0.1875 to 0.1875
- candidate_final_weights: bfloat16 [512, 256], replicated, may hold values from -0.25 to 0.25
Outputs:
- loss: float32 [], replicated
- grad_user_first: float32 [1024, 512], replicated
- grad_user_second: float32 [512, 256], replicated
- grad_item_first: float32 [1024, 512], replicated
- grad_item_second: float32 [512, 256], replicated
Inputs may be any that keep to these rules, and one draw needn't show every extreme that they name: correct_candidate_index[u] indexes the items of u's group in the order of the steps.
All inputs are finite; a program needn't handle non-finite values.
Results may differ from a plain program's by a relative error of at most 0.015.
Values may be sent and summed in bfloat16 or wider, within the bound.
A program may use at most 128 MiB of HBM per device.

v0:
```python
import jax
import jax.numpy as jnp
from jax import lax
from jax.sharding import PartitionSpec as P

EPS = 1e-06


def tower_forward(feats, first, second):
    pre = jnp.dot(feats, first, preferred_element_type=jnp.float32)
    hidden = jax.nn.relu(pre).astype(jnp.bfloat16)
    out = jnp.dot(hidden, second, preferred_element_type=jnp.float32)
    inv = lax.rsqrt(jnp.mean(out * out, axis=-1, keepdims=True) + EPS)
    return ((out * inv).astype(jnp.bfloat16), (pre, hidden, out, inv))


def tower_backward(feats, second, saved, grad_vec):
    pre, hidden, out, inv = saved
    grad = grad_vec.astype(jnp.float32)
    normed = out * inv
    grad_out = (inv * (grad - normed * jnp.mean(grad * normed, axis=-1, keepdims=True))).astype(
        jnp.bfloat16
    )
    grad_second = jnp.dot(hidden.T, grad_out, preferred_element_type=jnp.float32)
    grad_hidden = jnp.dot(grad_out, second.T, preferred_element_type=jnp.float32)
    grad_pre = jnp.where(pre > 0, grad_hidden, 0.0).astype(jnp.bfloat16)
    grad_first = jnp.dot(feats.T, grad_pre, preferred_element_type=jnp.float32)
    return (grad_first, grad_second)


def positive_pair_logit(
    shopper_vector, gathered_entries, affinity_sharpness, correct_candidate_index, resident_table
):
    latent_code = shopper_vector.shape[-1]
    coolness_fp32_number = affinity_sharpness.astype(jnp.float32)
    affinity_matrix = (
        coolness_fp32_number[:, None]
        * jnp.einsum(
            "ue,ie->ui", shopper_vector, gathered_entries, preferred_element_type=jnp.float32
        )
        / latent_code
    )
    lse = jax.nn.logsumexp(affinity_matrix, axis=1)
    columns = lax.broadcasted_iota(jnp.int32, affinity_matrix.shape, 1)
    target_column = columns == correct_candidate_index[:, None]
    picked = jnp.sum(jnp.where(target_column, affinity_matrix, 0.0), axis=1)
    softmax_likelihood = jnp.exp(affinity_matrix - lse[:, None])
    sensitivity_of_affinities = (
        (softmax_likelihood - target_column.astype(jnp.float32))
        * (coolness_fp32_number / (latent_code * resident_table))[:, None]
    ).astype(jnp.bfloat16)
    customer_derivative = jnp.dot(
        sensitivity_of_affinities, gathered_entries, preferred_element_type=jnp.float32
    )
    return (lse, sensitivity_of_affinities, customer_derivative, jnp.sum(lse - picked))


def body(
    customer_inputs,
    candidate_inputs,
    affinity_sharpness,
    correct_candidate_index,
    customer_initial_weights,
    customer_final_weights,
    candidate_initial_weights,
    candidate_final_weights,
):
    resident_table = customer_inputs.shape[0]
    shopper_vector, user_saved = tower_forward(
        customer_inputs, customer_initial_weights, customer_final_weights
    )
    offered_thing_vector, item_saved = tower_forward(
        candidate_inputs, candidate_initial_weights, candidate_final_weights
    )
    latent_code = shopper_vector.shape[-1]
    gathered_entries = lax.all_gather(offered_thing_vector, "row", axis=0, tiled=True)
    lse, sensitivity_of_affinities, customer_derivative, loss_local = positive_pair_logit(
        shopper_vector,
        gathered_entries,
        affinity_sharpness,
        correct_candidate_index,
        resident_table,
    )
    all_users, all_scales = (
        lax.all_gather(shopper_vector, "row", axis=0, tiled=True),
        lax.all_gather(affinity_sharpness, "row", axis=0, tiled=True),
    )
    all_positive = lax.all_gather(correct_candidate_index, "row", axis=0, tiled=True)
    all_lse = lax.all_gather(lse, "row", axis=0, tiled=True)
    coolness_fp32_number = all_scales.astype(jnp.float32)
    affinity_matrix = (
        coolness_fp32_number[:, None]
        * jnp.einsum(
            "ue,ie->ui", all_users, offered_thing_vector, preferred_element_type=jnp.float32
        )
        / latent_code
    )
    start = lax.axis_index("row") * resident_table
    columns = lax.broadcasted_iota(jnp.int32, affinity_matrix.shape, 1) + start
    target_column = columns == all_positive[:, None]
    softmax_likelihood = jnp.exp(affinity_matrix - all_lse[:, None])
    group_dlogits = (
        (softmax_likelihood - target_column.astype(jnp.float32))
        * (coolness_fp32_number / (latent_code * resident_table))[:, None]
    ).astype(jnp.bfloat16)
    candidate_derivative = jnp.einsum(
        "ui,ue->ie", group_dlogits, all_users, preferred_element_type=jnp.float32
    )
    grad_user_first, grad_user_second = tower_backward(
        customer_inputs,
        customer_final_weights,
        user_saved,
        customer_derivative.astype(jnp.bfloat16),
    )
    grad_item_first, grad_item_second = tower_backward(
        candidate_inputs,
        candidate_final_weights,
        item_saved,
        candidate_derivative.astype(jnp.bfloat16),
    )
    summed = lax.psum(
        (grad_user_first, grad_user_second, grad_item_first, grad_item_second, loss_local),
        ("row", "col"),
    )
    users_total = resident_table * lax.axis_size("row") * lax.axis_size("col")
    return (summed[4] / users_total, summed[0], summed[1], summed[2], summed[3])


def solution(mesh):
    placed = (
        P(("row", "col"), None),
        P(("row", "col"), None),
        P(("row", "col")),
        P(("row", "col")),
        P(),
        P(),
        P(),
        P(),
    )
    return jax.shard_map(
        body, mesh=mesh, in_specs=placed, out_specs=(P(), P(), P(), P(), P()), check_vma=False
    )
```

profile of v0, /device:TPU:0, one launch (start us, length us, event | category | flops | bytes accessed | tf_op | source)
XLA Modules:
  0.0 292.9 jit_solution(12754401451739418101)
XLA Ops:
  7.2 0.0 copy-start
  7.2 0.0 copy-start.12
  7.2 0.0 all-gather.3.cloned.1.call-start
  7.2 3.3 %fusion.26 = f32[1024,512]{1,0:T(8,128)S(1)} fusion(bf16[1024,1024]{1,0:T(8,128)(2,1)} %param.9, bf16[1024,512]{1,0:T(8,128)(2,1)} %param.14), kind=kOutput, calls=%fused_computation.56 | convolution fusion | flops 1073741824 | bytes 5242880 | tf_op jit(solution)/shard_map/dot_general | solution.py:10
  10.5 1.3 copy-done.3
  11.8 0.0 copy-done.12
  11.8 0.5 multiply_reduce_fusion
  12.4 0.9 multiply_convert_fusion.5
  13.3 0.0 all-gather.3.cloned.1.call-update
  13.3 0.0 copy-start.11
  13.3 0.0 all-gather.5.cloned.1.call-start
  13.4 2.5 fusion.25
  15.9 0.0 copy-start.4
  15.9 1.3 copy-done.4
  17.2 0.5 multiply_reduce_fusion.1
  17.7 0.0 copy-start.1
  17.7 0.9 copy-done.1
  18.7 0.9 multiply_convert_fusion.6
  19.6 0.0 all-gather.5.cloned.1.call-update
  19.6 0.0 all-reduce.3.cloned.1.call-start
  19.7 14.1 %all_gather.16 = bf16[4096]{0:T(1024)(128)(2,1)S(1)} all-gather(bf16[1024]{0:T(1024)(128)(2,1)S(1)} %copy-done.14), channel_id=1, replica_groups=mesh['row'=4,'col'=8] {'row'}, dimensions={0}, use_global_device_ids=true | all-gather | bytes 10240 | tf_op jit(solution)/shard_map/all_gather | solution.py:86
  33.8 13.6 %all_gather.19 = s32[4096]{0:T(1024)S(1)} all-gather(s32[1024]{0:T(1024)S(1)} %copy-done.15), channel_id=1, replica_groups=mesh['row'=4,'col'=8] {'row'}, dimensions={0}, use_global_device_ids=true | all-gather | bytes 20480 | tf_op jit(solution)/shard_map/all_gather | solution.py:88
  47.4 14.8 %all-gather.3.cloned.1.call-done = bf16[4096,256]{0,1:T(8,128)(2,1)} async-done(((bf16[1024,256]{0,1:T(8,128)(2,1)}), bf16[4096,256]{0,1:T(8,128)(2,1)}) %all-gather.3.cloned.1.call-update) | async-done | bytes 2097168 | tf_op jit(solution)/shard_map/all_gather | solution.py:76
  62.2 4.3 %fusion = (f32[1024]{0:T(1024)S(1)}, f32[1024,4096]{1,0:T(8,128)S(1)}) fusion(f32[1024]{0:T(1024)S(1)} %convert_element_type.54, bf16[1024,256]{0,1:T(8,128)(2,1)} %multiply_convert_fusion.6, bf16[4096,256]{0,1:T(8,128)(2,1)} %all-gather.3.cloned.1.call-done), kind=kOutput, calls=%fused_computation.6 | convolution fusion | flops 2160065536 | bytes 19406848 | tf_op jit(solution)/shard_map/ue,ie->ui/dot_general | solution.py:38
  66.4 0.0 copy-start.2
  66.5 6.9 %select_reduce_fusion = (f32[1024]{0:T(1024)S(1)}, f32[1024]{0:T(1024)S(1)}) fusion(f32[1024,4096]{1,0:T(8,128)S(1)} %get-tuple-element.28, s32[1024]{0:T(1024)S(1)} %copy-done.15, f32[1024]{0:T(1024)S(1)} %convert_element_type.54, f32[1024]{0:T(1024)S(1)} %is-finite_select_fusion), kind=kLoop, calls=%fused_computation.2 | loop fusion | flops 29358080 | bytes 16797696 | tf_op jit(solution)/shard_map/reduce_sum | solution.py:46
  73.3 0.6 subtract_reduce_fusion
  74.0 13.8 %all_gather.18 = f32[4096]{0:T(1024)S(1)} all-gather(f32[1024]{0:T(1024)S(1)} %get-tuple-element.22), channel_id=1, replica_groups=mesh['row'=4,'col'=8] {'row'}, dimensions={0}, use_global_device_ids=true | all-gather | bytes 20480 | tf_op jit(solution)/shard_map/all_gather | solution.py:89
  87.8 7.9 %fusion.5 = (f32[1024]{0:T(1024)S(1)}, bf16[1024,256]{0,1:T(8,128)(2,1)S(1)}) fusion(f32[1024,256]{0,1:T(8,128)S(1)} %copy-done.2, f32[1024]{0:T(1024)S(1)} %add_rsqrt_fusion.1, bf16[4096,256]{0,1:T(8,128)(2,1)S(1)} %copy-done.6, f32[1024,4096]{1,0:T(8,128)S(1)} %get-tuple-element.28, f32[1024]{0:T(1024)S(1)} %broadcast_multiply_fusion.1, ...), kind=kOutput, calls=%fused_computation.21 | convolution fusion | flops 2182347776 | bytes 20471808 | tf_op jit(solution)/shard_map/dot_general | solution.py:52
  95.7 0.0 copy-start.5
  95.7 0.2 fusion.7
  95.9 0.0 copy-start.7
  96.0 0.8 copy-done.7
  96.7 0.8 copy-done.5
  97.5 1.3 fusion.13
  98.8 4.7 %convolution_bitcast_fusion.1 = f32[1024,512]{0,1:T(8,128)} fusion(bf16[1024,1024]{1,0:T(8,128)(2,1)S(1)} %copy-done, f32[1024,512]{1,0:T(8,128)} %copy-done.4, bf16[1024,256]{0,1:T(8,128)(2,1)} %copy-done.7, bf16[512,256]{1,0:T(8,128)(2,1)S(1)} %copy-done.11), kind=kOutput, calls=%fused_computation.14 | convolution fusion | flops 1343750144 | bytes 7077888 | tf_op jit(solution)/shard_map/dot_general | solution.py:27
  103.5 5.5 %all-gather.5.cloned.1.call-done = bf16[4096,256]{0,1:T(8,128)(2,1)} async-done(((bf16[1024,256]{0,1:T(8,128)(2,1)}), bf16[4096,256]{0,1:T(8,128)(2,1)}) %all-gather.5.cloned.1.call-update) | async-done | bytes 2097168 | tf_op jit(solution)/shard_map/all_gather | solution.py:85
  109.1 10.3 %fusion.8 = (f32[1024]{0:T(1024)S(1)}, bf16[1024,256]{0,1:T(8,128)(2,1)}) fusion(f32[1024,256]{0,1:T(8,128)S(1)} %get-tuple-element.26, f32[1024]{0:T(1024)S(1)} %add_rsqrt_fusion, bf16[4096,256]{0,1:T(8,128)(2,1)} %all-gather.5.cloned.1.call-done, f32[4096]{0:T(1024)S(1)} %broadcast_multiply_fusion, s32[1024]{0:T(1024)S(1)} %iota_add_fusion, ...), kind=kOutput, calls=%fused_computation.24 | convolution fusion | flops 4330355712 | bytes 3747840 | tf_op jit(solution)/shard_map/ui,ue->ie/dot_general | solution.py:106
  119.4 2.1 fusion.10
  121.4 5.4 %convolution_bitcast_fusion = f32[1024,512]{0,1:T(8,128)} fusion(bf16[1024,1024]{1,0:T(8,128)(2,1)} %param.9, f32[1024,512]{1,0:T(8,128)} %copy-done.3, bf16[1024,256]{0,1:T(8,128)(2,1)} %fusion.10, bf16[512,256]{1,0:T(8,128)(2,1)S(1)} %copy-done.13), kind=kOutput, calls=%fused_computation.13 | convolution fusion | flops 1343750144 | bytes 7077888 | tf_op jit(solution)/shard_map/dot_general | solution.py:27
  126.8 2.9 fusion.15
  129.7 0.0 all-reduce.3.cloned.1.call-update
  129.7 39.7 %psum.35 = f32[]{:T(128)} all-reduce(f32[]{:T(128)} %get-tuple-element.21), channel_id=1, replica_groups=mesh['row'=4,'col'=8] {'row','col'}, use_global_device_ids=true, to_apply=%region_6.7 | all-reduce | flops 1 | bytes 8 | tf_op jit(solution)/shard_map/psum | solution.py:121
  170.0 107.8 %all-reduce.3.cloned.1.call-done = (f32[1024,512]{0,1:T(8,128)}, f32[512,256]{1,0:T(8,128)}, f32[1024,512]{0,1:T(8,128)}, f32[512,256]{1,0:T(8,128)}) async-done(((f32[1024,512]{0,1:T(8,128)}, f32[512,256]{1,0:T(8,128)}, f32[1024,512]{0,1:T(8,128)}, f32[512,256]{1,0:T(8,128)}), (f32[1024,512]{0,1:T(8,128)}, f32[512,256]{1,0:T(8,128)}, f32[1024,512]{0,1:T(8,128)}, ...) | async-done | bytes 5242896 | tf_op jit(solution)/shard_map/psum | solution.py:121
  277.8 2.9 copy.15
  280.7 3.0 %copy.16 = f32[1024,512]{1,0:T(8,128)} copy(f32[1024,512]{0,1:T(8,128)} %get-tuple-element.19) | data formatting | bytes 4194304
  283.6 0.8 copy.21
  284.4 0.8 copy.22
  (28 shorter events, 0.1 us)
Async XLA Ops:
  7.2 6.2 %copy-start = (bf16[1024,1024]{1,0:T(8,128)(2,1)S(1)}, bf16[1024,1024]{1,0:T(8,128)(2,1)}, u32[]{:S(2)}) copy-start(bf16[1024,1024]{1,0:T(8,128)(2,1)} %param.8) | copy-start | bytes 6291460
  7.2 4.7 %copy-start.12 = (bf16[512,256]{1,0:T(8,128)(2,1)S(1)}, bf16[512,256]{1,0:T(8,128)(2,1)}, u32[]{:S(2)}) copy-start(bf16[512,256]{1,0:T(8,128)(2,1)} %param.15) | copy-start | bytes 786436
  7.2 55.0 %all-gather.3.cloned.1.call-start = ((), (), s32[]{:S(2)}) async-start(), calls=%async_computation | async-start | bytes 2621440 | tf_op jit(solution)/shard_map/all_gather | solution.py:76
  10.5 1.3 copy-start.3
  13.3 3.9 %copy-start.11 = (bf16[512,256]{1,0:T(8,128)(2,1)S(1)}, bf16[512,256]{1,0:T(8,128)(2,1)}, u32[]{:S(2)}) copy-start(bf16[512,256]{1,0:T(8,128)(2,1)} %param.13) | copy-start | bytes 786436
  13.3 95.8 %all-gather.5.cloned.1.call-start = ((), (), s32[]{:S(2)}) async-start(), calls=%async_computation.1 | async-start | bytes 2621440 | tf_op jit(solution)/shard_map/all_gather | solution.py:85
  15.9 1.3 copy-start.4
  17.2 2.4 copy-start.14
  17.2 16.6 %copy-start.15 = (s32[1024]{0:T(1024)S(1)}, s32[1024]{0:T(1024)}, u32[]{:S(2)}) copy-start(s32[1024]{0:T(1024)} %param.11) | copy-start | bytes 12292
  17.7 1.0 copy-start.1
  19.6 258.2 %all-reduce.3.cloned.1.call-start = ((), (), s32[]{:S(2)}) async-start(), calls=%async_computation.2 | async-start | bytes 10485760 | tf_op jit(solution)/shard_map/psum | solution.py:121
  66.4 21.3 %copy-start.2 = (f32[1024,256]{0,1:T(8,128)S(1)}, f32[1024,256]{0,1:T(8,128)}, u32[]{:S(2)}) copy-start(f32[1024,256]{0,1:T(8,128)} %copy-done.1) | copy-start | bytes 3145732
  66.4 21.3 %copy-start.6 = (bf16[4096,256]{0,1:T(8,128)(2,1)S(1)}, bf16[4096,256]{0,1:T(8,128)(2,1)}, u32[]{:S(2)}) copy-start(bf16[4096,256]{0,1:T(8,128)(2,1)} %all-gather.3.cloned.1.call-done) | copy-start | bytes 6291460
  95.7 1.8 copy-start.5
  95.9 0.8 copy-start.7
  119.3 2.1 copy-start.13
  121.4 5.4 %copy-start.8 = (bf16[1024,256]{0,1:T(8,128)(2,1)S(1)}, bf16[1024,256]{0,1:T(8,128)(2,1)}, u32[]{:S(2)}) copy-start(bf16[1024,256]{0,1:T(8,128)(2,1)} %fusion.10) | copy-start | bytes 1572868
  280.7 3.0 %copy-start.10 = (f32[512,256]{1,0:T(8,128)S(1)}, f32[512,256]{1,0:T(8,128)}, u32[]{:S(2)}) copy-start(f32[512,256]{1,0:T(8,128)} %get-tuple-element.35) | copy-start | bytes 1572868
  280.7 3.8 %copy-start.9 = (f32[512,256]{1,0:T(8,128)S(1)}, f32[512,256]{1,0:T(8,128)}, u32[]{:S(2)}) copy-start(f32[512,256]{1,0:T(8,128)} %get-tuple-element.37) | copy-start | bytes 1572868
Sparse Core Ops, SparseCore 0:
  13.4 48.7 all-gather.2
  64.3 44.7 all-gather.4
  129.8 147.9 all-reduce.2
where the time goes:
time: 293 us
  waiting for transfers between devices  128 us (44%)
  blocking collectives  81.1 us (28%)
  matrix products  43.5 us (15%)
  between operations  15.7 us (5%)
  local copies, waits for them, and re-layouts  12.6 us (4%)
  other arithmetic  11.6 us (4%)
    psum x1, waiting for transfers between devices, body(): lax.psum((grad_user_first, grad_user_second, grad_item_first, grad_item_s...  108 us
    psum x1, blocking collectives, body(): lax.psum((grad_user_first, grad_user_second, grad_item_first, grad_item_s...  39.7 us
    all_gather x1, waiting for transfers between devices, body(): lax.all_gather(offered_thing_vector, 'row', axis=0, tiled=True)  14.8 us
    all_gather x1, blocking collectives, body(): lax.all_gather(affinity_sharpness, 'row', axis=0, tiled=True)  14.1 us
    all_gather x1, blocking collectives, body(): all_lse = lax.all_gather(lse, 'row', axis=0, tiled=True)  13.8 us
    all_gather x1, blocking collectives, body(): lax.all_gather(correct_candidate_index, 'row', axis=0, tiled=True)  13.6 us
    unnamed x36, local copies, waits for them, and re-layouts  12.6 us
    dot_general x1, matrix products, body(): jnp.einsum('ui,ue->ie', group_dlogits, all_users, preferred_element_type=...  10.3 us
  transfers between devices with their start and end apart: 3, of which 3 were waited for; matrix products, arithmetic and copies ran while one was open for 10% of the time, Pallas kernels for 0%

commit v1 on v0

--- a/solution.py
+++ b/solution.py
@@ -119,8 +119,11 @@
         candidate_derivative.astype(jnp.bfloat16),
     )
     summed = lax.psum(
-        (grad_user_first, grad_user_second, grad_item_first, grad_item_second, loss_local),
-        ("row", "col"),
+        lax.psum(
+            (grad_user_first, grad_user_second, grad_item_first, grad_item_second, loss_local),
+            "col",
+        ),
+        "row",
     )
     users_total = resident_table * lax.axis_size("row") * lax.axis_size("col")
     return (summed[4] / users_total, summed[0], summed[1], summed[2], summed[3])

time: 293 us -> 428 us (1.46)
  waiting for transfers between devices: 128 us -> 276 us
  blocking collectives: 81.1 us -> 68.1 us
    psum x0 -> x1, waiting for transfers between devices: none -> 164 us  [body(): lax.psum(lax.psum((grad_user_first, grad_user_second, grad_item_first, gr...]
    psum x1, blocking collectives: 39.7 us -> 13.4 us  [body(): lax.psum((grad_user_first, grad_user_second, grad_item_first, grad_item_s...]
    psum x1, waiting for transfers between devices: 108 us -> 91.4 us  [body(): lax.psum((grad_user_first, grad_user_second, grad_item_first, grad_item_s...]
    psum x0 -> x1, blocking collectives: none -> 13.3 us  [body(): lax.psum(lax.psum((grad_user_first, grad_user_second, grad_item_first, gr...]
  transfers between devices with their start and end apart: 3 -> 4, of which waited for: 3 -> 4; matrix products, arithmetic and copies ran while one was open for 10% -> 7% of each run, Pallas kernels for 0% -> 0%
where the time goes in v1:
time: 428 us
  waiting for transfers between devices  276 us (64%)
  blocking collectives  68.1 us (16%)
  matrix products  43.5 us (10%)
  between operations  15.8 us (4%)
  local copies, waits for them, and re-layouts  12.6 us (3%)
  other arithmetic  11.6 us (3%)
    psum x1, waiting for transfers between devices, body(): lax.psum(lax.psum((grad_user_first, grad_user_second, grad_item_first, gr...  164 us
    psum x1, waiting for transfers between devices, body(): lax.psum((grad_user_first, grad_user_second, grad_item_first, grad_item_s...  91.4 us
    all_gather x1, waiting for transfers between devices, body(): lax.all_gather(offered_thing_vector, 'row', axis=0, tiled=True)  14.9 us
    all_gather x1, blocking collectives, body(): lax.all_gather(affinity_sharpness, 'row', axis=0, tiled=True)  14.1 us
    all_gather x1, blocking collectives, body(): all_lse = lax.all_gather(lse, 'row', axis=0, tiled=True)  13.8 us
    all_gather x1, blocking collectives, body(): lax.all_gather(correct_candidate_index, 'row', axis=0, tiled=True)  13.5 us
    psum x1, blocking collectives, body(): lax.psum((grad_user_first, grad_user_second, grad_item_first, grad_item_s...  13.4 us
    psum x1, blocking collectives, body(): lax.psum(lax.psum((grad_user_first, grad_user_second, grad_item_first, gr...  13.3 us
  transfers between devices with their start and end apart: 4, of which 4 were waited for; matrix products, arithmetic and copies ran while one was open for 7% of the time, Pallas kernels for 0%

profile of v1, /device:TPU:0, one launch (start us, length us, event | category | flops | bytes accessed | tf_op | source)
XLA Modules:
  0.0 428.0 jit_solution(17085692951126846788)
XLA Ops:
  7.2 0.0 copy-start
  7.2 0.0 copy-start.12
  7.2 0.0 all-gather.3.cloned.1.call-start
  7.2 3.3 fusion.26
  10.5 1.3 copy-done.3
  11.8 0.5 multiply_reduce_fusion
  12.4 0.9 multiply_convert_fusion.5
  13.3 0.0 all-gather.3.cloned.1.call-update
  13.3 0.0 copy-start.11
  13.3 0.0 all-gather.5.cloned.1.call-start
  13.4 2.5 fusion.25
  15.9 0.0 copy-start.4
  15.9 1.3 copy-done.4
  17.2 0.5 multiply_reduce_fusion.1
  17.7 0.9 copy-done.1
  18.7 0.9 multiply_convert_fusion.6
  19.6 0.0 all-gather.5.cloned.1.call-update
  19.6 0.0 all-reduce.5.cloned.1.call-start
  19.7 14.1 %all_gather.16 = bf16[4096]{0:T(1024)(128)(2,1)S(1)} all-gather(bf16[1024]{0:T(1024)(128)(2,1)S(1)} %copy-done.14), channel_id=1, replica_groups=mesh['row'=4,'col'=8] {'row'}, dimensions={0}, use_global_device_ids=true | all-gather | bytes 10240 | tf_op jit(solution)/shard_map/all_gather | solution.py:86
  33.8 13.5 %all_gather.19 = s32[4096]{0:T(1024)S(1)} all-gather(s32[1024]{0:T(1024)S(1)} %copy-done.15), channel_id=1, replica_groups=mesh['row'=4,'col'=8] {'row'}, dimensions={0}, use_global_device_ids=true | all-gather | bytes 20480 | tf_op jit(solution)/shard_map/all_gather | solution.py:88
  47.3 14.9 %all-gather.3.cloned.1.call-done = bf16[4096,256]{0,1:T(8,128)(2,1)} async-done(((bf16[1024,256]{0,1:T(8,128)(2,1)}), bf16[4096,256]{0,1:T(8,128)(2,1)}) %all-gather.3.cloned.1.call-update) | async-done | bytes 2097168 | tf_op jit(solution)/shard_map/all_gather | solution.py:76
  62.2 4.3 fusion
  66.4 0.0 copy-start.2
  66.5 6.9 %select_reduce_fusion = (f32[1024]{0:T(1024)S(1)}, f32[1024]{0:T(1024)S(1)}) fusion(f32[1024,4096]{1,0:T(8,128)S(1)} %get-tuple-element.32, s32[1024]{0:T(1024)S(1)} %copy-done.15, f32[1024]{0:T(1024)S(1)} %convert_element_type.54, f32[1024]{0:T(1024)S(1)} %is-finite_select_fusion), kind=kLoop, calls=%fused_computation.2 | loop fusion | flops 29358080 | bytes 16797696 | tf_op jit(solution)/shard_map/reduce_sum | solution.py:46
  73.3 0.6 subtract_reduce_fusion
  74.0 13.8 %all_gather.18 = f32[4096]{0:T(1024)S(1)} all-gather(f32[1024]{0:T(1024)S(1)} %get-tuple-element.26), channel_id=1, replica_groups=mesh['row'=4,'col'=8] {'row'}, dimensions={0}, use_global_device_ids=true | all-gather | bytes 20480 | tf_op jit(solution)/shard_map/all_gather | solution.py:89
  87.8 7.9 %fusion.5 = (f32[1024]{0:T(1024)S(1)}, bf16[1024,256]{0,1:T(8,128)(2,1)S(1)}) fusion(f32[1024,256]{0,1:T(8,128)S(1)} %copy-done.2, f32[1024]{0:T(1024)S(1)} %add_rsqrt_fusion.1, bf16[4096,256]{0,1:T(8,128)(2,1)S(1)} %copy-done.6, f32[1024,4096]{1,0:T(8,128)S(1)} %get-tuple-element.32, f32[1024]{0:T(1024)S(1)} %broadcast_multiply_fusion.1, ...), kind=kOutput, calls=%fused_computation.21 | convolution fusion | flops 2182347776 | bytes 20471808 | tf_op jit(solution)/shard_map/dot_general | solution.py:52
  95.7 0.2 fusion.7
  96.0 0.8 copy-done.7
  96.7 0.8 copy-done.5
  97.5 1.3 fusion.13
  98.8 4.7 %convolution_bitcast_fusion.1 = f32[1024,512]{0,1:T(8,128)} fusion(bf16[1024,1024]{1,0:T(8,128)(2,1)S(1)} %copy-done, f32[1024,512]{1,0:T(8,128)} %copy-done.4, bf16[1024,256]{0,1:T(8,128)(2,1)} %copy-done.7, bf16[512,256]{1,0:T(8,128)(2,1)S(1)} %copy-done.11), kind=kOutput, calls=%fused_computation.14 | convolution fusion | flops 1343750144 | bytes 7077888 | tf_op jit(solution)/shard_map/dot_general | solution.py:27
  103.5 5.6 %all-gather.5.cloned.1.call-done = bf16[4096,256]{0,1:T(8,128)(2,1)} async-done(((bf16[1024,256]{0,1:T(8,128)(2,1)}), bf16[4096,256]{0,1:T(8,128)(2,1)}) %all-gather.5.cloned.1.call-update) | async-done | bytes 2097168 | tf_op jit(solution)/shard_map/all_gather | solution.py:85
  109.1 10.3 %fusion.8 = (f32[1024]{0:T(1024)S(1)}, bf16[1024,256]{0,1:T(8,128)(2,1)}) fusion(f32[1024,256]{0,1:T(8,128)S(1)} %get-tuple-element.30, f32[1024]{0:T(1024)S(1)} %add_rsqrt_fusion, bf16[4096,256]{0,1:T(8,128)(2,1)} %all-gather.5.cloned.1.call-done, f32[4096]{0:T(1024)S(1)} %broadcast_multiply_fusion, s32[1024]{0:T(1024)S(1)} %iota_add_fusion, ...), kind=kOutput, calls=%fused_computation.24 | convolution fusion | flops 4330355712 | bytes 3747840 | tf_op jit(solution)/shard_map/ui,ue->ie/dot_general | solution.py:106
  119.4 2.1 fusion.10
  121.4 5.4 %convolution_bitcast_fusion = f32[1024,512]{0,1:T(8,128)} fusion(bf16[1024,1024]{1,0:T(8,128)(2,1)} %param.9, f32[1024,512]{1,0:T(8,128)} %copy-done.3, bf16[1024,256]{0,1:T(8,128)(2,1)} %fusion.10, bf16[512,256]{1,0:T(8,128)(2,1)S(1)} %copy-done.13), kind=kOutput, calls=%fused_computation.13 | convolution fusion | flops 1343750144 | bytes 7077888 | tf_op jit(solution)/shard_map/dot_general | solution.py:27
  126.8 2.9 fusion.15
  129.7 0.0 all-reduce.5.cloned.1.call-update
  129.7 0.0 all-reduce.7.cloned.1.call-start
  129.8 91.4 %all-reduce.5.cloned.1.call-done = (f32[1024,512]{0,1:T(8,128)}, f32[512,256]{1,0:T(8,128)}, f32[1024,512]{0,1:T(8,128)}, f32[512,256]{1,0:T(8,128)}) async-done(((f32[1024,512]{0,1:T(8,128)}, f32[512,256]{1,0:T(8,128)}, f32[1024,512]{0,1:T(8,128)}, f32[512,256]{1,0:T(8,128)}), (f32[1024,512]{0,1:T(8,128)}, f32[512,256]{1,0:T(8,128)}, f32[1024,512]{0,1:T(8,128)}, ...) | async-done | bytes 5242896 | tf_op jit(solution)/shard_map/psum | solution.py:122
  221.1 0.0 all-reduce.7.cloned.1.call-update
  221.2 13.4 %psum.70 = f32[]{:T(128)} all-reduce(f32[]{:T(128)} %get-tuple-element.25), channel_id=1, replica_groups=mesh['row'=4,'col'=8] {'col'}, use_global_device_ids=true, to_apply=%region_6.7 | all-reduce | flops 1 | bytes 8 | tf_op jit(solution)/shard_map/psum | solution.py:122
  234.6 13.3 %psum.71 = f32[]{:T(128)} all-reduce(f32[]{:T(128)} %psum.70), channel_id=1, replica_groups=mesh['row'=4,'col'=8] {'row'}, use_global_device_ids=true, to_apply=%region_7.8 | all-reduce | flops 1 | bytes 8 | tf_op jit(solution)/shard_map/psum | solution.py:121
  248.5 164.4 %all-reduce.7.cloned.1.call-done = (f32[1024,512]{0,1:T(8,128)}, f32[512,256]{1,0:T(8,128)}, f32[1024,512]{0,1:T(8,128)}, f32[512,256]{1,0:T(8,128)}) async-done(((f32[1024,512]{0,1:T(8,128)}, f32[512,256]{1,0:T(8,128)}, f32[1024,512]{0,1:T(8,128)}, f32[512,256]{1,0:T(8,128)}), (f32[1024,512]{0,1:T(8,128)}, f32[512,256]{1,0:T(8,128)}, f32[1024,512]{0,1:T(8,128)}, ...) | async-done | bytes 5242896 | tf_op jit(solution)/shard_map/psum | solution.py:121
  412.9 2.9 copy.15
  415.8 3.0 copy.16
  418.8 0.8 copy.25
  419.6 0.8 copy.26
  (32 shorter events, 0.1 us)
Async XLA Ops:
  7.2 6.2 %copy-start = (bf16[1024,1024]{1,0:T(8,128)(2,1)S(1)}, bf16[1024,1024]{1,0:T(8,128)(2,1)}, u32[]{:S(2)}) copy-start(bf16[1024,1024]{1,0:T(8,128)(2,1)} %param.8) | copy-start | bytes 6291460
  7.2 4.7 %copy-start.12 = (bf16[512,256]{1,0:T(8,128)(2,1)S(1)}, bf16[512,256]{1,0:T(8,128)(2,1)}, u32[]{:S(2)}) copy-start(bf16[512,256]{1,0:T(8,128)(2,1)} %param.15) | copy-start | bytes 786436
  7.2 55.0 %all-gather.3.cloned.1.call-start = ((), (), s32[]{:S(2)}) async-start(), calls=%async_computation | async-start | bytes 2621440 | tf_op jit(solution)/shard_map/all_gather | solution.py:76
  10.5 1.3 copy-start.3
  13.3 3.9 copy-start.11
  13.3 95.8 %all-gather.5.cloned.1.call-start = ((), (), s32[]{:S(2)}) async-start(), calls=%async_computation.1 | async-start | bytes 2621440 | tf_op jit(solution)/shard_map/all_gather | solution.py:85
  15.9 1.3 copy-start.4
  17.2 2.4 copy-start.14
  17.2 16.6 %copy-start.15 = (s32[1024]{0:T(1024)S(1)}, s32[1024]{0:T(1024)}, u32[]{:S(2)}) copy-start(s32[1024]{0:T(1024)} %param.11) | copy-start | bytes 12292
  17.7 1.0 copy-start.1
  19.6 201.6 %all-reduce.5.cloned.1.call-start = ((), (), s32[]{:S(2)}) async-start(), calls=%async_computation.2 | async-start | bytes 10485760 | tf_op jit(solution)/shard_map/psum | solution.py:122
  66.4 21.3 %copy-start.2 = (f32[1024,256]{0,1:T(8,128)S(1)}, f32[1024,256]{0,1:T(8,128)}, u32[]{:S(2)}) copy-start(f32[1024,256]{0,1:T(8,128)} %copy-done.1) | copy-start | bytes 3145732
  66.4 21.3 %copy-start.6 = (bf16[4096,256]{0,1:T(8,128)(2,1)S(1)}, bf16[4096,256]{0,1:T(8,128)(2,1)}, u32[]{:S(2)}) copy-start(bf16[4096,256]{0,1:T(8,128)(2,1)} %all-gather.3.cloned.1.call-done) | copy-start | bytes 6291460
  95.7 1.8 copy-start.5
  95.9 0.8 copy-start.7
  119.4 2.1 copy-start.13
  121.4 5.4 %copy-start.8 = (bf16[1024,256]{0,1:T(8,128)(2,1)S(1)}, bf16[1024,256]{0,1:T(8,128)(2,1)}, u32[]{:S(2)}) copy-start(bf16[1024,256]{0,1:T(8,128)(2,1)} %fusion.10) | copy-start | bytes 1572868
  129.7 283.2 %all-reduce.7.cloned.1.call-start = ((), (), s32[]{:S(2)}) async-start(), calls=%async_computation.3 | async-start | bytes 10485760 | tf_op jit(solution)/shard_map/psum | solution.py:121
  415.8 3.0 copy-start.10
  415.8 3.8 copy-start.9
Sparse Core Ops, SparseCore 0:
  13.4 48.7 all-gather.2
  64.3 44.7 all-gather.4
  129.8 91.2 all-reduce.4
  223.6 189.2 all-reduce.6
